TPU v7x, 32 devices: a whole 2x2x4 slice. The times are simulated.
32 devices in a mesh: seq: 8 (over z, y), dp: 4 (over x, core).
Axes of the slice: x: 2, y: 2, z: 4, core: 2. Of those that a mesh axis runs over, the one named last changes fastest.
Arguments:
- tokens: bfloat16 [4, 2048, 2048], P('dp', 'seq'), may hold values from -6 to 6
- query_weight: bfloat16 [2048, 2048], P(None, 'seq'), may hold values from -0.125 to 0.125
- key_rows: bfloat16 [4, 2048, 2048], P('dp', 'seq'), may hold values from -6 to 6
- value_rows: bfloat16 [4, 2048, 2048], P('dp', 'seq'), may hold values from -6 to 6
- out_grad: bfloat16 [4, 2048, 2048], P('dp', 'seq'), may hold values from -6 to 6
Outputs:
- attended: bfloat16 [4, 2048, 2048], P('dp', 'seq')
- key_grad: bfloat16 [4, 2048, 2048], P('dp', 'seq')
- value_grad: bfloat16 [4, 2048, 2048], P('dp', 'seq')
- weight_grad: float32 [2048, 2048], P('seq')
All inputs are finite; a program needn't handle non-finite values.
Results may differ from a plain program's by a relative error of at most 0.0058.
Values may be sent and summed in bfloat16 or wider, within the bound.
No kernel may reach another device: no remote copies, remote signals or barrier semaphores. Data moves between devices by JAX's collectives and lax.ppermute only.
A program may use at most 320 MiB of HBM per device.

v0:
```python
import math
import jax
import jax.numpy as jnp
from jax import lax
from jax.sharding import PartitionSpec as P

DH = 128


def carried_in(value, axis, join, neutral, backward):
    count, mine = (lax.axis_size(axis), lax.axis_index(axis))
    pieces = lax.all_gather(value, axis)
    if backward:
        pieces = pieces[::-1]
        mine = count - 1 - mine
    total = jnp.full_like(value, 0) + jnp.asarray(neutral, value.dtype)

    def step(position, total):
        longer = join(total, pieces[position])
        return jnp.where(position < mine, longer, total)

    return lax.fori_loop(0, count - 1, step, total)


def pair_sum(earlier, later):
    return jax.tree.map(jnp.add, earlier, later)


def body(tokens, query_weight, key_rows, value_rows, out_grad):
    row_count = tokens.shape[1]
    hidden_width = key_rows.shape[2]
    head_count = hidden_width // DH
    seq_count = lax.axis_size("seq")
    factor = 1.0 / math.sqrt(DH * row_count * seq_count)
    local_tokens = tokens[0]
    query_rows = jnp.dot(
        local_tokens,
        lax.all_gather(query_weight, "seq", axis=1, tiled=True),
        preferred_element_type=jnp.float32,
    ).astype(jnp.bfloat16)
    query_heads = query_rows.reshape(row_count, head_count, DH)
    key_heads = key_rows[0].reshape(row_count, head_count, DH)
    value_heads = value_rows[0].reshape(row_count, head_count, DH)
    grad_heads = out_grad[0].reshape(row_count, head_count, DH)
    block_kv = jnp.einsum(
        "rhd,rhe->hde", key_heads, value_heads, preferred_element_type=jnp.float32
    )
    block_qg = jnp.einsum(
        "rhd,rhe->hde", query_heads, grad_heads, preferred_element_type=jnp.float32
    )
    zero_state = jnp.zeros_like(block_kv)
    prefix_state = carried_in(block_kv, "seq", pair_sum, zero_state, False)
    suffix_state = carried_in(block_qg, "seq", pair_sum, zero_state, True)
    prefix_half = prefix_state.astype(jnp.bfloat16)
    suffix_half = suffix_state.astype(jnp.bfloat16)
    lower_mask = (
        lax.broadcasted_iota(jnp.int32, (row_count, row_count), 0)
        >= lax.broadcasted_iota(jnp.int32, (row_count, row_count), 1)
    )[None]
    key_scores = jnp.where(
        lower_mask,
        factor
        * jnp.einsum("ihd,jhd->hij", query_heads, key_heads, preferred_element_type=jnp.float32),
        0.0,
    ).astype(jnp.bfloat16)
    grad_scores = jnp.where(
        lower_mask,
        factor
        * jnp.einsum("ihe,jhe->hij", grad_heads, value_heads, preferred_element_type=jnp.float32),
        0.0,
    ).astype(jnp.bfloat16)
    attended = jnp.einsum(
        "hij,jhe->ihe", key_scores, value_heads, preferred_element_type=jnp.float32
    ) + factor * jnp.einsum(
        "ihd,hde->ihe", query_heads, prefix_half, preferred_element_type=jnp.float32
    )
    query_grad = jnp.einsum(
        "hij,jhd->ihd", grad_scores, key_heads, preferred_element_type=jnp.float32
    ) + factor * jnp.einsum(
        "ihe,hde->ihd", grad_heads, prefix_half, preferred_element_type=jnp.float32
    )
    key_grad = jnp.einsum(
        "hij,ihd->jhd", grad_scores, query_heads, preferred_element_type=jnp.float32
    ) + factor * jnp.einsum(
        "jhe,hde->jhd", value_heads, suffix_half, preferred_element_type=jnp.float32
    )
    value_grad = jnp.einsum(
        "hij,ihe->jhe", key_scores, grad_heads, preferred_element_type=jnp.float32
    ) + factor * jnp.einsum(
        "jhd,hde->jhe", key_heads, suffix_half, preferred_element_type=jnp.float32
    )
    attended = attended.reshape(1, row_count, hidden_width).astype(jnp.bfloat16)
    query_grad = query_grad.reshape(row_count, hidden_width).astype(jnp.bfloat16)
    key_grad = key_grad.reshape(1, row_count, hidden_width).astype(jnp.bfloat16)
    value_grad = value_grad.reshape(1, row_count, hidden_width).astype(jnp.bfloat16)
    grad_shard = lax.psum_scatter(
        lax.dot_general(
            local_tokens, query_grad, (((0,), (0,)), ((), ())), preferred_element_type=jnp.float32
        ),
        "seq",
        scatter_dimension=0,
        tiled=True,
    )
    weight_grad = lax.psum(grad_shard, "dp")
    return (attended, key_grad, value_grad, weight_grad)


def solution(mesh):
    return jax.shard_map(
        body,
        mesh=mesh,
        in_specs=(
            P("dp", "seq", None),
            P(None, "seq"),
            P("dp", "seq", None),
            P("dp", "seq", None),
            P("dp", "seq", None),
        ),
        out_specs=(
            P("dp", "seq", None),
            P("dp", "seq", None),
            P("dp", "seq", None),
            P("seq", None),
        ),
        check_vma=False,
    )
```

profile of v0, /device:TPU:0, one launch (start us, length us, event | category | flops | bytes accessed | tf_op | source)
XLA Modules:
  0.0 732.2 jit_solution(10739160041827640124)
XLA Ops:
  10.7 1.6 copy.34
  13.8 2.5 copy.58
  16.3 121.4 %all-gather.6.cloned.1.call-done = bf16[2048,2048]{1,0:T(8,128)(2,1)} async-done(((bf16[2048,256]{1,0:T(8,128)(2,1)}), bf16[2048,2048]{1,0:T(8,128)(2,1)}) %all-gather.6.cloned.1.call-update) | async-done | bytes 8388624 | tf_op jit(solution)/shard_map/all_gather | solution.py:38
  137.7 6.7 convolution_convert_fusion
  145.9 3.2 fusion.11
  149.3 2.1 select_convert_fusion
  152.8 2.2 fusion.24
  155.0 108.1 %all-gather.8.cloned.1.call-done = f32[128,128,128]{2,1,0:T(8,128)} async-done(((f32[16,128,128]{2,1,0:T(8,128)}), f32[128,128,128]{2,1,0:T(8,128)}) %all-gather.8.cloned.1.call-update) | async-done | bytes 8388624 | tf_op jit(solution)/shard_map/all_gather | solution.py:12
  263.1 11.6 %while.28 = (s32[]{:T(128)}, f32[16,128,128]{2,1,0:T(8,128)S(1)}, s32[]{:T(128)}, f32[8,16,128,128]{3,2,1,0:T(8,128)}, s32[]{:T(128)}, /*index=5*/s32[]{:T(128)}) while((s32[]{:T(128)}, f32[16,128,128]{2,1,0:T(8,128)S(1)}, s32[]{:T(128)}, f32[8,16,128,128]{3,2,1,0:T(8,128)}, s32[]{:T(128)}, /*index=5*/s32[]{:T(128)}) %tuple.81), condition=%wide.region_1.2_spmd.clone, body=%wide.region_0.1_spmd.clone.sunk | while | flops 786436 | bytes 3145821 | solution.py:22
  264.7 1.6 add_select_fusion.4
  269.6 1.7 add_select_fusion.4
  271.3 1.7 add_select_fusion.4
  273.0 1.7 add_select_fusion.4
  274.8 2.4 fusion
  277.2 8.1 %convolution_bitcast_fusion = f32[2048,2048]{0,1:T(8,128)} fusion(bf16[256,2048]{0,1:T(8,128)(2,1)S(1)} %bitcast.79, bf16[1,256,2048]{2,1,0:T(8,128)(2,1)S(1)} %copy-done), kind=kOutput, calls=%fused_computation.2 | convolution fusion | flops 2147483648 | bytes 18874368 | tf_op jit(solution)/shard_map/dot_general | solution.py:97
  285.6 2.4 select_convert_fusion.1
  291.5 2.4 copy.49
  293.8 3.4 fusion.23
  297.2 90.8 %all-gather.10.cloned.1.call-done = f32[128,128,128]{2,1,0:T(8,128)} async-done(((f32[16,128,128]{2,1,0:T(8,128)}), f32[128,128,128]{2,1,0:T(8,128)}) %all-gather.10.cloned.1.call-update) | async-done | bytes 8388624 | tf_op jit(solution)/shard_map/all_gather | solution.py:12
  387.9 7.7 %rev.3 = f32[8,16,128,128]{3,2,1,0:T(8,128)} reverse(f32[8,16,128,128]{3,2,1,0:T(8,128)} %bitcast.78), dimensions={0} | reverse | bytes 16777216 | tf_op jit(solution)/shard_map/rev | solution.py:14
  395.7 11.4 %while.29 = (s32[]{:T(128)}, f32[16,128,128]{2,1,0:T(8,128)S(1)}, s32[]{:T(128)}, f32[8,16,128,128]{3,2,1,0:T(8,128)}, s32[]{:T(128)}, /*index=5*/s32[]{:T(128)}) while((s32[]{:T(128)}, f32[16,128,128]{2,1,0:T(8,128)S(1)}, s32[]{:T(128)}, f32[8,16,128,128]{3,2,1,0:T(8,128)}, s32[]{:T(128)}, /*index=5*/s32[]{:T(128)}) %tuple.68), condition=%wide.region_3.4_spmd.clone, body=%wide.region_2.3_spmd.clone.sunk | while | flops 786436 | bytes 3145821 | solution.py:22
  395.7 1.6 add_select_fusion.5
  397.3 1.6 add_select_fusion.5
  399.0 1.6 add_select_fusion.5
  402.2 1.6 add_select_fusion.5
  403.8 1.6 add_select_fusion.5
  405.5 1.6 add_select_fusion.5
  407.1 263.0 %reduce-scatter.2.cloned.1.call-done = f32[256,2048]{0,1:T(8,128)} async-done(((f32[2048,2048]{0,1:T(8,128)}), f32[256,2048]{0,1:T(8,128)}) %reduce-scatter.2.cloned.1.call-update) | async-done | bytes 2097168 | tf_op jit(solution)/shard_map/reduce_scatter | solution.py:96
  670.1 3.1 add_convert_fusion
  673.2 2.4 copy.50
  679.9 43.0 %all-reduce.2.cloned.1.call-done = f32[256,2048]{0,1:T(8,128)} async-done(((f32[256,2048]{0,1:T(8,128)}), f32[256,2048]{0,1:T(8,128)}) %all-reduce.2.cloned.1.call-update) | async-done | bytes 2097168 | tf_op jit(solution)/shard_map/psum | solution.py:104
  722.8 2.9 copy.52
  (52 shorter events, 22.2 us)
Async XLA Ops:
  7.2 130.6 %copy-start = (bf16[1,256,2048]{2,1,0:T(8,128)(2,1)S(1)}, bf16[1,256,2048]{2,1,0:T(8,128)(2,1)}, u32[]{:S(2)}) copy-start(bf16[1,256,2048]{2,1,0:T(8,128)(2,1)} %param.9) | copy-start | bytes 3145732
  7.2 2.3 copy-start.12
  7.2 130.5 %all-gather.6.cloned.1.call-start = ((), (), s32[]{:S(2)}) async-start(), calls=%async_computation.1 | async-start | bytes 9437184 | tf_op jit(solution)/shard_map/all_gather | solution.py:38
  7.9 255.2 %all-gather.8.cloned.1.call-start = ((), (), s32[]{:S(2)}) async-start(), calls=%async_computation.4 | async-start | bytes 9437184 | tf_op jit(solution)/shard_map/all_gather | solution.py:12
  12.3 1.5 copy-start.6
  13.8 374.2 %all-gather.10.cloned.1.call-start = ((), (), s32[]{:S(2)}) async-start(), calls=%async_computation.5 | async-start | bytes 9437184 | tf_op jit(solution)/shard_map/all_gather | solution.py:12
  145.9 3.3 copy-start.2
  149.2 520.9 %reduce-scatter.2.cloned.1.call-start = ((), (), s32[]{:S(2)}) async-start(), calls=%async_computation.2 | async-start | bytes 18874368 | tf_op jit(solution)/shard_map/reduce_scatter | solution.py:96
  149.3 3.5 copy-start.7
  151.5 1.3 copy-start.11
  285.3 437.5 %all-reduce.2.cloned.1.call-start = ((), (), s32[]{:S(2)}) async-start(), calls=%async_computation.3 | async-start | bytes 4194304 | tf_op jit(solution)/shard_map/psum | solution.py:104
  288.0 1.4 copy-start.9
  288.0 2.0 copy-start.3
  291.5 2.4 copy-start.4
  673.2 2.4 copy-start.8
  675.5 1.3 copy-start.5
  675.5 2.3 copy-start.10
  678.4 47.3 %copy-start.1 = (bf16[1,256,2048]{2,1,0:T(8,128)(2,1)S(1)}, bf16[1,256,2048]{2,1,0:T(8,128)(2,1)}, u32[]{:S(2)}) copy-start(bf16[1,256,2048]{2,1,0:T(8,128)(2,1)} %param.9) | copy-start | bytes 3145732
Sparse Core Ops, SparseCore 0:
  10.0 127.6 all-gather.5
  140.4 122.6 all-gather.7
  265.3 122.6 all-gather.9
  391.6 278.4 reduce-scatter.1
  672.3 50.4 all-reduce.1
where the time goes:
time: 733 us; the launch traced here: 732 us
  waiting for transfers between devices  627 us (86%)
  matrix products  38.5 us (5%)
  local copies, waits for them, and re-layouts  29.3 us (4%)
  other arithmetic  22.7 us (3%)
  between operations  14 us (2%)
    reduce_scatter x1, waiting for transfers between devices, body(): lax.psum_scatter(lax.dot_general(local_tokens, query_grad, (((0,), (0,)),...  263 us
    all_gather x2, waiting for transfers between devices, carried_in(): pieces = lax.all_gather(value, axis)  199 us
    all_gather x1, waiting for transfers between devices, body(): lax.all_gather(query_weight, 'seq', axis=1, tiled=True)  121 us
    psum x1, waiting for transfers between devices, body(): weight_grad = lax.psum(grad_shard, 'dp')  43 us
    select_n x14, other arithmetic, step(): return jnp.where(position < mine, longer, total)  22.7 us
    unnamed x33, local copies, waits for them, and re-layouts  18.5 us
  transfers between devices with their start and end apart: 5, of which 5 were waited for; matrix products, arithmetic and copies ran while one was open for 11% of the time, Pallas kernels for 0%

commit v1 on v0

--- a/solution.py
+++ b/solution.py
@@ -101,7 +101,11 @@
         scatter_dimension=0,
         tiled=True,
     )
-    weight_grad = lax.psum(grad_shard, "dp")
+    weight_grad = grad_shard
+    for hop in (1, 2):
+        weight_grad = weight_grad + lax.ppermute(
+            weight_grad, "dp", [(dev, dev ^ hop) for dev in range(4)]
+        )
     return (attended, key_grad, value_grad, weight_grad)
 
 

time: 733 us -> 747 us (1.019)
  other arithmetic: 22.7 us -> 30.3 us
    psum x1 -> x0, waiting for transfers between devices: 43 us -> none  [body(): weight_grad = lax.psum(grad_shard, 'dp')]
    all_gather x2, waiting for transfers between devices: 199 us -> 232 us  [carried_in(): pieces = lax.all_gather(value, axis)]
    ppermute x0 -> x2, waiting for transfers between devices: none -> 24.8 us  [body(): lax.ppermute(weight_grad, 'dp', [(dev, dev ^ hop) for dev in range(4)])]
    all_gather x1, waiting for transfers between devices: 121 us -> 103 us  [body(): lax.all_gather(query_weight, 'seq', axis=1, tiled=True)]
    add x0 -> x2, other arithmetic: none -> 7.72 us  [body(): weight_grad + lax.ppermute(weight_grad, 'dp', [(dev, dev ^ hop) for dev i...]
    reduce_scatter x1, waiting for transfers between devices: 263 us -> 271 us  [body(): lax.psum_scatter(lax.dot_general(local_tokens, query_grad, (((0,), (0,)),...]
  transfers between devices with their start and end apart: 5 -> 6, of which waited for: 5 -> 5; matrix products, arithmetic and copies ran while one was open for 11% -> 10% of each run, Pallas kernels for 0% -> 0%
where the time goes in v1:
time: 747 us; the launch traced here: 745 us
  waiting for transfers between devices  631 us (84%)
  matrix products  38.9 us (5%)
  other arithmetic  30.3 us (4%)
  local copies, waits for them, and re-layouts  29 us (4%)
  between operations  14 us (2%)
    reduce_scatter x1, waiting for transfers between devices, body(): lax.psum_scatter(lax.dot_general(local_tokens, query_grad, (((0,), (0,)),...  271 us
    all_gather x2, waiting for transfers between devices, carried_in(): pieces = lax.all_gather(value, axis)  232 us
    all_gather x1, waiting for transfers between devices, body(): lax.all_gather(query_weight, 'seq', axis=1, tiled=True)  103 us
    ppermute x2, waiting for transfers between devices, body(): lax.ppermute(weight_grad, 'dp', [(dev, dev ^ hop) for dev in range(4)])  24.8 us
    select_n x14, other arithmetic, step(): return jnp.where(position < mine, longer, total)  22.5 us
    unnamed x33, local copies, waits for them, and re-layouts  18.2 us
  transfers between devices with their start and end apart: 6, of which 5 were waited for; matrix products, arithmetic and copies ran while one was open for 10% of the time, Pallas kernels for 0%

profile of v1, /device:TPU:0, one launch (start us, length us, event | category | flops | bytes accessed | tf_op | source)
XLA Modules:
  0.0 745.5 jit_solution(2825717203893851360)
XLA Ops:
  10.1 1.6 copy.34
  14.0 2.5 copy.58
  16.5 2.1 select_convert_fusion
  20.0 2.2 fusion.24
  22.2 118.3 %all-gather.8.cloned.1.call-done = f32[128,128,128]{2,1,0:T(8,128)} async-done(((f32[16,128,128]{2,1,0:T(8,128)}), f32[128,128,128]{2,1,0:T(8,128)}) %all-gather.8.cloned.1.call-update) | async-done | bytes 8388624 | tf_op jit(solution)/shard_map/all_gather | solution.py:12
  140.5 11.5 %while.28 = (s32[]{:T(128)}, f32[16,128,128]{2,1,0:T(8,128)S(1)}, s32[]{:T(128)}, f32[8,16,128,128]{3,2,1,0:T(8,128)}, s32[]{:T(128)}, /*index=5*/s32[]{:T(128)}) while((s32[]{:T(128)}, f32[16,128,128]{2,1,0:T(8,128)S(1)}, s32[]{:T(128)}, f32[8,16,128,128]{3,2,1,0:T(8,128)}, s32[]{:T(128)}, /*index=5*/s32[]{:T(128)}) %tuple.79), condition=%wide.region_1.2_spmd.clone, body=%wide.region_0.1_spmd.clone.sunk | while | flops 786436 | bytes 3145821 | solution.py:22
  143.8 1.6 add_select_fusion.4
  145.4 1.6 add_select_fusion.4
  147.0 1.7 add_select_fusion.4
  148.7 1.7 add_select_fusion.4
  150.4 1.6 add_select_fusion.4
  152.1 2.5 fusion
  154.6 8.1 %convolution_bitcast_fusion = f32[2048,2048]{0,1:T(8,128)} fusion(bf16[256,2048]{0,1:T(8,128)(2,1)S(1)} %bitcast.79, bf16[1,256,2048]{2,1,0:T(8,128)(2,1)S(1)} %copy-done), kind=kOutput, calls=%fused_computation.2 | convolution fusion | flops 2147483648 | bytes 18874368 | tf_op jit(solution)/shard_map/dot_general | solution.py:97
  162.9 102.8 %all-gather.6.cloned.1.call-done = bf16[2048,2048]{1,0:T(8,128)(2,1)} async-done(((bf16[2048,256]{1,0:T(8,128)(2,1)}), bf16[2048,2048]{1,0:T(8,128)(2,1)}) %all-gather.6.cloned.1.call-update) | async-done | bytes 8388624 | tf_op jit(solution)/shard_map/all_gather | solution.py:38
  265.7 6.7 convolution_convert_fusion
  273.9 3.3 fusion.11
  277.2 270.7 %reduce-scatter.2.cloned.1.call-done = f32[256,2048]{0,1:T(8,128)} async-done(((f32[2048,2048]{0,1:T(8,128)}), f32[256,2048]{0,1:T(8,128)}) %reduce-scatter.2.cloned.1.call-update) | async-done | bytes 2097168 | tf_op jit(solution)/shard_map/reduce_scatter | solution.py:96
  548.0 2.4 select_convert_fusion.1
  553.9 2.4 copy.49
  556.2 3.7 fusion.23
  559.9 113.7 %all-gather.10.cloned.1.call-done = f32[128,128,128]{2,1,0:T(8,128)} async-done(((f32[16,128,128]{2,1,0:T(8,128)}), f32[128,128,128]{2,1,0:T(8,128)}) %all-gather.10.cloned.1.call-update) | async-done | bytes 8388624 | tf_op jit(solution)/shard_map/all_gather | solution.py:12
  673.6 7.8 %rev.3 = f32[8,16,128,128]{3,2,1,0:T(8,128)} reverse(f32[8,16,128,128]{3,2,1,0:T(8,128)} %bitcast.78), dimensions={0} | reverse | bytes 16777216 | tf_op jit(solution)/shard_map/rev | solution.py:14
  681.3 3.8 add.81
  686.6 11.3 %while.29 = (s32[]{:T(128)}, f32[16,128,128]{2,1,0:T(8,128)S(1)}, s32[]{:T(128)}, f32[8,16,128,128]{3,2,1,0:T(8,128)}, s32[]{:T(128)}, /*index=5*/s32[]{:T(128)}) while((s32[]{:T(128)}, f32[16,128,128]{2,1,0:T(8,128)S(1)}, s32[]{:T(128)}, f32[8,16,128,128]{3,2,1,0:T(8,128)}, s32[]{:T(128)}, /*index=5*/s32[]{:T(128)}) %tuple.68), condition=%wide.region_3.4_spmd.clone, body=%wide.region_2.3_spmd.clone.sunk | while | flops 786436 | bytes 3145821 | solution.py:22
  689.9 1.6 add_select_fusion.5
  693.1 1.6 add_select_fusion.5
  696.3 1.6 add_select_fusion.5
  697.9 3.1 add_convert_fusion
  701.0 2.4 copy.50
  707.3 24.8 %collective-permute-done.1 = f32[256,2048]{0,1:T(8,128)} collective-permute-done((f32[256,2048]{0,1:T(8,128)}, f32[256,2048]{0,1:T(8,128)}, u32[]{:S(2)}, u32[]{:S(2)}) %collective-permute-start.1) | collective-permute-done | bytes 2097184 | tf_op jit(solution)/shard_map/ppermute | solution.py:106
  732.1 3.9 add.82
  736.0 2.9 copy.52
  (55 shorter events, 26.6 us)
Async XLA Ops:
  7.2 147.4 %copy-start = (bf16[1,256,2048]{2,1,0:T(8,128)(2,1)S(1)}, bf16[1,256,2048]{2,1,0:T(8,128)(2,1)}, u32[]{:S(2)}) copy-start(bf16[1,256,2048]{2,1,0:T(8,128)(2,1)} %param.9) | copy-start | bytes 3145732
  7.2 1.7 copy-start.12
  7.2 133.3 %all-gather.8.cloned.1.call-start = ((), (), s32[]{:S(2)}) async-start(), calls=%async_computation.3 | async-start | bytes 9437184 | tf_op jit(solution)/shard_map/all_gather | solution.py:12
  11.7 1.5 copy-start.6
  13.2 252.5 %all-gather.6.cloned.1.call-start = ((), (), s32[]{:S(2)}) async-start(), calls=%async_computation.1 | async-start | bytes 9437184 | tf_op jit(solution)/shard_map/all_gather | solution.py:38
  13.9 534.0 %reduce-scatter.2.cloned.1.call-start = ((), (), s32[]{:S(2)}) async-start(), calls=%async_computation.2 | async-start | bytes 18874368 | tf_op jit(solution)/shard_map/reduce_scatter | solution.py:96
  16.5 3.5 copy-start.7
  18.6 1.3 copy-start.11
  162.6 510.9 %all-gather.10.cloned.1.call-start = ((), (), s32[]{:S(2)}) async-start(), calls=%async_computation.4 | async-start | bytes 9437184 | tf_op jit(solution)/shard_map/all_gather | solution.py:12
  273.9 3.3 copy-start.2
  548.0 133.4 %collective-permute-start = (f32[256,2048]{0,1:T(8,128)}, f32[256,2048]{0,1:T(8,128)}, u32[]{:S(2)}, u32[]{:S(2)}) collective-permute-start(f32[256,2048]{0,1:T(8,128)} %reduce-scatter.2.cloned.1.call-done), channel_id=1, source_target_pairs={{0,1},{1,0},{2,3},{3,2},{4,5},{5,4},{6,7},{7,6},{8,9},{9,8},{10,11... | collective-permute-start | bytes 6291464 | tf_op jit(solution)/shard_map/ppermute | solution.py:106
  550.4 1.4 copy-start.9
  550.4 2.0 copy-start.3
  553.9 2.4 copy-start.4
  685.2 47.0 %collective-permute-start.1 = (f32[256,2048]{0,1:T(8,128)}, f32[256,2048]{0,1:T(8,128)}, u32[]{:S(2)}, u32[]{:S(2)}) collective-permute-start(f32[256,2048]{0,1:T(8,128)} %add.81), channel_id=1, source_target_pairs={{0,2},{1,3},{2,0},{3,1},{4,6},{5,7},{6,4},{7,5},{8,10},{9,11},{10,... | collective-permute-start | bytes 6291464 | tf_op jit(solution)/shard_map/ppermute | solution.py:106
  701.0 2.4 copy-start.8
  703.3 1.2 copy-start.5
  703.3 1.9 copy-start.10
  732.1 6.8 copy-start.1
Sparse Core Ops, SparseCore 0:
  13.3 127.1 all-gather.7
  142.6 123.1 all-gather.5
  269.5 278.4 reduce-scatter.1
  549.9 123.5 all-gather.9
